TPU v7x, 512 devices: a whole 4x8x8 slice. The times are simulated.
512 devices in a mesh: phase: 16 (over z, core), rows: 32 (over y, x).
Axes of the slice: x: 4, y: 8, z: 8, core: 2. Of those that a mesh axis runs over, the one named last changes fastest.
Arguments:
- start: bfloat16 [16, 32768, 256], P('phase', 'rows')
- blocks: bfloat16 [16, 256, 4, 128, 128], P('phase', 'rows')
- cols: int32 [16, 256, 4], P('phase', 'rows'), may hold values from 0 to 255, as said below
- counts: int32 [16, 256], P('phase', 'rows'), may hold values from 1 to 4, as said below
Outputs:
- basis: float32 [16, 32768, 256], P('phase', 'rows')
- factor: float32 [16, 256, 256], P('phase')
Inputs may be any that keep to these rules, and one draw needn't show every extreme that they name: cols[q, i, 0] = i; the other slots of block row i name distinct block rows (i + o) mod 256 with 1 <= |o| <= 2. Block row i of section q uses its first counts[q, i] slots; every section has a block row that uses all 4.
All inputs are finite; a program needn't handle non-finite values.
Results may differ from a plain program's by a relative error of at most 0.012.
Values may be sent and summed in bfloat16 or wider, within the bound.
No kernel may reach another device: no remote copies, remote signals or barrier semaphores. Data moves between devices by JAX's collectives and lax.ppermute only.
A program may use at most 64 MiB of HBM per device.

v0:
```python
import jax
import jax.numpy as jnp
from jax import lax
from jax.sharding import PartitionSpec as P

HB = 2


def with_halo(array, sides, width):
    for axis, dim in sides:
        peers, length = (lax.axis_size(axis), array.shape[dim])
        up = [(i, (i + 1) % peers) for i in range(peers)]
        down = [(j, i) for i, j in up]
        last = lax.slice_in_dim(array, length - width, length, axis=dim)
        leading = lax.slice_in_dim(array, 0, width, axis=dim)
        before = lax.ppermute(last, axis, up)
        after = lax.ppermute(leading, axis, down)
        array = jnp.concatenate([before, array, after], axis=dim)
    return array


def passed_along(value, axis, steps):
    count = lax.axis_size(axis)
    pairs = [(source, (source + steps) % count) for source in range(count)]
    return lax.ppermute(value, axis, pairs)


def body(start, blocks, cols, counts):
    block_rows = blocks.shape[1]
    slot_count = blocks.shape[2]
    tile_size = blocks.shape[3]
    rows_here = start.shape[1]
    owners = lax.axis_size("rows")
    sections = lax.axis_size("phase")
    total_blocks = block_rows * owners
    first_block = lax.axis_index("rows") * block_rows
    local_index = jnp.mod(cols[0] - first_block + HB, total_blocks)
    live_slots = jnp.arange(slot_count, dtype=jnp.int32)[None, :] < counts[0][:, None]
    zero_value = jnp.zeros((), jnp.bfloat16)
    kept_blocks = jnp.where(live_slots[:, :, None, None], blocks[0], zero_value)
    rim_rows = HB * tile_size

    def advance(current):
        columns = current.shape[1]
        extended = with_halo(current, (("rows", 0),), rim_rows)
        row_tiles = extended.reshape(block_rows + 2 * HB, tile_size, columns)
        picked = row_tiles[local_index]
        product = jnp.einsum(
            "ijab,ijbk->iak", kept_blocks, picked, preferred_element_type=jnp.float32
        )
        return product.reshape(rows_here, columns).astype(jnp.bfloat16)

    def turn_one(turn_index, current):
        return passed_along(advance(current), "phase", 1)

    arrived = lax.fori_loop(0, sections, turn_one, start[0])
    gram_term = lax.dot_general(
        arrived, arrived, (((0,), (0,)), ((), ())), preferred_element_type=jnp.float32
    )
    gram_total = lax.psum(gram_term.astype(jnp.bfloat16), "rows").astype(jnp.float32) / (
        rows_here * owners
    )
    lower_factor = jnp.linalg.cholesky(gram_total)
    basis_out = jax.scipy.linalg.solve_triangular(
        lower_factor, arrived.astype(jnp.float32).T, lower=True
    ).T
    return (basis_out[None], lower_factor.T[None])


def solution(mesh):
    placed = (
        P("phase", "rows", None),
        P("phase", "rows", None, None, None),
        P("phase", "rows", None),
        P("phase", "rows"),
    )
    return jax.shard_map(
        body,
        mesh=mesh,
        in_specs=placed,
        out_specs=(P("phase", "rows", None), P("phase", None, None)),
        check_vma=False,
    )
```

profile of v0, /device:TPU:2, one launch (start us, length us, event | category | flops | bytes accessed | tf_op | source)
XLA Modules:
  0.0 634.1 jit_solution(17564700713426844968)
XLA Ops:
  10.4 398.1 %while.11 = (s32[]{:T(128)}, bf16[1024,256]{1,0:T(8,128)(2,1)S(1)}, s32[8,4]{0,1:T(4,128)S(1)}, bf16[8,4,128,128]{3,2,1,0:T(8,128)(2,1)}, s32[]{:T(128)}) while((s32[]{:T(128)}, bf16[1024,256]{1,0:T(8,128)(2,1)S(1)}, s32[8,4]{0,1:T(4,128)S(1)}, bf16[8,4,128,128]{3,2,1,0:T(8,128)(2,1)}, s32[]{:T(128)}) %tuple.54), condition=%wide.region_1.2_spmd, body=%wide.region_0.1_spmd.sunk | while | flops 271058016 | bytes 13112501 | solution.py:56
  10.4 7.8 %collective-permute-start = (bf16[256,256]{1,0:T(8,128)(2,1)S(1)}, bf16[256,256]{1,0:T(8,128)(2,1)S(1)}, u32[]{:S(2)}, u32[]{:S(2)}) collective-permute-start(bf16[256,256]{1,0:T(8,128)(2,1)S(1)} %get-tuple-element.117), channel_id=1, source_target_pairs={{1,0},{2,1},{3,2},{4,3},{5,4},{6,5},{7,6},{8,7},{9,8},{10,9},{11,1... | collective-permute-start | bytes 393224 | tf_op jit(solution)/shard_map/while/body/eval_jaxpr/ppermute | solution.py:17
  27.6 13.0 %collective-permute-done.2 = bf16[1024,256]{1,0:T(8,128)(2,1)S(1)} collective-permute-done((bf16[1024,256]{1,0:T(8,128)(2,1)S(1)}, bf16[1024,256]{1,0:T(8,128)(2,1)S(1)}, u32[]{:S(2)}, u32[]{:S(2)}) %collective-permute-start.2) | collective-permute-done | bytes 524320 | tf_op jit(solution)/shard_map/while/body/eval_jaxpr/ppermute | solution.py:25
  40.6 6.4 %collective-permute-start = (bf16[256,256]{1,0:T(8,128)(2,1)S(1)}, bf16[256,256]{1,0:T(8,128)(2,1)S(1)}, u32[]{:S(2)}, u32[]{:S(2)}) collective-permute-start(bf16[256,256]{1,0:T(8,128)(2,1)S(1)} %get-tuple-element.117), channel_id=1, source_target_pairs={{1,0},{2,1},{3,2},{4,3},{5,4},{6,5},{7,6},{8,7},{9,8},{10,9},{11,1... | collective-permute-start | bytes 393224 | tf_op jit(solution)/shard_map/while/body/eval_jaxpr/ppermute | solution.py:17
  56.4 9.8 %collective-permute-done.2 = bf16[1024,256]{1,0:T(8,128)(2,1)S(1)} collective-permute-done((bf16[1024,256]{1,0:T(8,128)(2,1)S(1)}, bf16[1024,256]{1,0:T(8,128)(2,1)S(1)}, u32[]{:S(2)}, u32[]{:S(2)}) %collective-permute-start.2) | collective-permute-done | bytes 524320 | tf_op jit(solution)/shard_map/while/body/eval_jaxpr/ppermute | solution.py:25
  66.2 5.2 collective-permute-start
  80.9 9.8 %collective-permute-done.2 = bf16[1024,256]{1,0:T(8,128)(2,1)S(1)} collective-permute-done((bf16[1024,256]{1,0:T(8,128)(2,1)S(1)}, bf16[1024,256]{1,0:T(8,128)(2,1)S(1)}, u32[]{:S(2)}, u32[]{:S(2)}) %collective-permute-start.2) | collective-permute-done | bytes 524320 | tf_op jit(solution)/shard_map/while/body/eval_jaxpr/ppermute | solution.py:25
  90.7 5.2 collective-permute-start
  105.3 9.8 %collective-permute-done.2 = bf16[1024,256]{1,0:T(8,128)(2,1)S(1)} collective-permute-done((bf16[1024,256]{1,0:T(8,128)(2,1)S(1)}, bf16[1024,256]{1,0:T(8,128)(2,1)S(1)}, u32[]{:S(2)}, u32[]{:S(2)}) %collective-permute-start.2) | collective-permute-done | bytes 524320 | tf_op jit(solution)/shard_map/while/body/eval_jaxpr/ppermute | solution.py:25
  115.1 5.2 collective-permute-start
  129.8 9.8 %collective-permute-done.2 = bf16[1024,256]{1,0:T(8,128)(2,1)S(1)} collective-permute-done((bf16[1024,256]{1,0:T(8,128)(2,1)S(1)}, bf16[1024,256]{1,0:T(8,128)(2,1)S(1)}, u32[]{:S(2)}, u32[]{:S(2)}) %collective-permute-start.2) | collective-permute-done | bytes 524320 | tf_op jit(solution)/shard_map/while/body/eval_jaxpr/ppermute | solution.py:25
  154.2 9.8 %collective-permute-done.2 = bf16[1024,256]{1,0:T(8,128)(2,1)S(1)} collective-permute-done((bf16[1024,256]{1,0:T(8,128)(2,1)S(1)}, bf16[1024,256]{1,0:T(8,128)(2,1)S(1)}, u32[]{:S(2)}, u32[]{:S(2)}) %collective-permute-start.2) | collective-permute-done | bytes 524320 | tf_op jit(solution)/shard_map/while/body/eval_jaxpr/ppermute | solution.py:25
  164.0 5.2 collective-permute-start
  178.7 9.8 %collective-permute-done.2 = bf16[1024,256]{1,0:T(8,128)(2,1)S(1)} collective-permute-done((bf16[1024,256]{1,0:T(8,128)(2,1)S(1)}, bf16[1024,256]{1,0:T(8,128)(2,1)S(1)}, u32[]{:S(2)}, u32[]{:S(2)}) %collective-permute-start.2) | collective-permute-done | bytes 524320 | tf_op jit(solution)/shard_map/while/body/eval_jaxpr/ppermute | solution.py:25
  203.1 9.8 %collective-permute-done.2 = bf16[1024,256]{1,0:T(8,128)(2,1)S(1)} collective-permute-done((bf16[1024,256]{1,0:T(8,128)(2,1)S(1)}, bf16[1024,256]{1,0:T(8,128)(2,1)S(1)}, u32[]{:S(2)}, u32[]{:S(2)}) %collective-permute-start.2) | collective-permute-done | bytes 524320 | tf_op jit(solution)/shard_map/while/body/eval_jaxpr/ppermute | solution.py:25
  212.9 5.2 collective-permute-start
  227.5 9.8 %collective-permute-done.2 = bf16[1024,256]{1,0:T(8,128)(2,1)S(1)} collective-permute-done((bf16[1024,256]{1,0:T(8,128)(2,1)S(1)}, bf16[1024,256]{1,0:T(8,128)(2,1)S(1)}, u32[]{:S(2)}, u32[]{:S(2)}) %collective-permute-start.2) | collective-permute-done | bytes 524320 | tf_op jit(solution)/shard_map/while/body/eval_jaxpr/ppermute | solution.py:25
  252.0 9.8 %collective-permute-done.2 = bf16[1024,256]{1,0:T(8,128)(2,1)S(1)} collective-permute-done((bf16[1024,256]{1,0:T(8,128)(2,1)S(1)}, bf16[1024,256]{1,0:T(8,128)(2,1)S(1)}, u32[]{:S(2)}, u32[]{:S(2)}) %collective-permute-start.2) | collective-permute-done | bytes 524320 | tf_op jit(solution)/shard_map/while/body/eval_jaxpr/ppermute | solution.py:25
  261.8 5.2 collective-permute-start
  276.4 9.8 %collective-permute-done.2 = bf16[1024,256]{1,0:T(8,128)(2,1)S(1)} collective-permute-done((bf16[1024,256]{1,0:T(8,128)(2,1)S(1)}, bf16[1024,256]{1,0:T(8,128)(2,1)S(1)}, u32[]{:S(2)}, u32[]{:S(2)}) %collective-permute-start.2) | collective-permute-done | bytes 524320 | tf_op jit(solution)/shard_map/while/body/eval_jaxpr/ppermute | solution.py:25
  300.9 9.8 %collective-permute-done.2 = bf16[1024,256]{1,0:T(8,128)(2,1)S(1)} collective-permute-done((bf16[1024,256]{1,0:T(8,128)(2,1)S(1)}, bf16[1024,256]{1,0:T(8,128)(2,1)S(1)}, u32[]{:S(2)}, u32[]{:S(2)}) %collective-permute-start.2) | collective-permute-done | bytes 524320 | tf_op jit(solution)/shard_map/while/body/eval_jaxpr/ppermute | solution.py:25
  310.7 5.2 collective-permute-start
  325.3 9.8 %collective-permute-done.2 = bf16[1024,256]{1,0:T(8,128)(2,1)S(1)} collective-permute-done((bf16[1024,256]{1,0:T(8,128)(2,1)S(1)}, bf16[1024,256]{1,0:T(8,128)(2,1)S(1)}, u32[]{:S(2)}, u32[]{:S(2)}) %collective-permute-start.2) | collective-permute-done | bytes 524320 | tf_op jit(solution)/shard_map/while/body/eval_jaxpr/ppermute | solution.py:25
  349.8 9.8 %collective-permute-done.2 = bf16[1024,256]{1,0:T(8,128)(2,1)S(1)} collective-permute-done((bf16[1024,256]{1,0:T(8,128)(2,1)S(1)}, bf16[1024,256]{1,0:T(8,128)(2,1)S(1)}, u32[]{:S(2)}, u32[]{:S(2)}) %collective-permute-start.2) | collective-permute-done | bytes 524320 | tf_op jit(solution)/shard_map/while/body/eval_jaxpr/ppermute | solution.py:25
  359.6 5.2 collective-permute-start
  374.2 9.8 %collective-permute-done.2 = bf16[1024,256]{1,0:T(8,128)(2,1)S(1)} collective-permute-done((bf16[1024,256]{1,0:T(8,128)(2,1)S(1)}, bf16[1024,256]{1,0:T(8,128)(2,1)S(1)}, u32[]{:S(2)}, u32[]{:S(2)}) %collective-permute-start.2) | collective-permute-done | bytes 524320 | tf_op jit(solution)/shard_map/while/body/eval_jaxpr/ppermute | solution.py:25
  398.7 9.8 %collective-permute-done.2 = bf16[1024,256]{1,0:T(8,128)(2,1)S(1)} collective-permute-done((bf16[1024,256]{1,0:T(8,128)(2,1)S(1)}, bf16[1024,256]{1,0:T(8,128)(2,1)S(1)}, u32[]{:S(2)}, u32[]{:S(2)}) %collective-permute-start.2) | collective-permute-done | bytes 524320 | tf_op jit(solution)/shard_map/while/body/eval_jaxpr/ppermute | solution.py:25
  409.5 151.6 %all-reduce.3.cloned.1.call-done = bf16[256,256]{0,1:T(8,128)(2,1)} async-done(((bf16[256,256]{0,1:T(8,128)(2,1)}), bf16[256,256]{0,1:T(8,128)(2,1)}) %all-reduce.3.cloned.1.call-update) | async-done | bytes 131088 | tf_op jit(solution)/shard_map/psum | solution.py:60
  563.2 11.7 %cholesky.50 = f32[128,128]{1,0:T(8,128)S(1)} custom-call(f32[128,128]{1,0:T(8,128)S(1)} %cholesky.118), custom_call_target="Cholesky" | custom-call | tf_op jit(solution)/shard_map/jit(cholesky)/cholesky | solution.py:63
  574.9 9.8 %custom-call.15 = f32[1,128,128]{1,2,0:T(8,128)S(1)} custom-call(f32[1,128,128]{2,1,0:T(8,128)S(1)} %get-tuple-element.62), custom_call_target="InvertDiagBlocksLowerTriangular" | custom-call | tf_op jit(solution)/shard_map/jit(cholesky)/cholesky | solution.py:63
  585.2 11.7 %cholesky.105 = f32[128,128]{1,0:T(8,128)S(1)} custom-call(f32[128,128]{1,0:T(8,128)S(1)} %convolution_subtract_fusion.1), custom_call_target="Cholesky" | custom-call | tf_op jit(solution)/shard_map/jit(cholesky)/cholesky | solution.py:63
  603.0 19.9 %custom-call.16 = f32[2,128,128]{1,2,0:T(8,128)S(1)} custom-call(f32[2,128,128]{2,1,0:T(8,128)S(1)} %get-tuple-element.32), custom_call_target="InvertDiagBlocksLowerTriangular" | custom-call | tf_op jit(solution)/shard_map/jit(_solve_triangular)/triangular_solve | solution.py:64
  (235 shorter events, 200.7 us)
Async XLA Ops:
  7.2 553.9 %all-reduce.3.cloned.1.call-start = ((), (), s32[]{:S(2)}) async-start(), calls=%async_computation | async-start | bytes 262144 | tf_op jit(solution)/shard_map/psum | solution.py:60
  10.4 10.3 %collective-permute-start = (bf16[256,256]{1,0:T(8,128)(2,1)S(1)}, bf16[256,256]{1,0:T(8,128)(2,1)S(1)}, u32[]{:S(2)}, u32[]{:S(2)}) collective-permute-start(bf16[256,256]{1,0:T(8,128)(2,1)S(1)} %get-tuple-element.117), channel_id=1, source_target_pairs={{1,0},{2,1},{3,2},{4,3},{5,4},{6,5},{7,6},{8,7},{9,8},{10,9},{11,1... | collective-permute-start | bytes 393224 | tf_op jit(solution)/shard_map/while/body/eval_jaxpr/ppermute | solution.py:17
  27.5 13.1 %collective-permute-start.2 = (bf16[1024,256]{1,0:T(8,128)(2,1)S(1)}, bf16[1024,256]{1,0:T(8,128)(2,1)S(1)}, u32[]{:S(2)}, u32[]{:S(2)}) collective-permute-start(bf16[1024,256]{1,0:T(8,128)(2,1)S(1)} %bitcast.85), channel_id=1, source_target_pairs={{0,32},{32,64},{64,96},{96,128},{128,160},{160,192},{192,224},{224... | collective-permute-start | bytes 1572872 | tf_op jit(solution)/shard_map/while/body/eval_jaxpr/ppermute | solution.py:25
  40.6 8.9 %collective-permute-start = (bf16[256,256]{1,0:T(8,128)(2,1)S(1)}, bf16[256,256]{1,0:T(8,128)(2,1)S(1)}, u32[]{:S(2)}, u32[]{:S(2)}) collective-permute-start(bf16[256,256]{1,0:T(8,128)(2,1)S(1)} %get-tuple-element.117), channel_id=1, source_target_pairs={{1,0},{2,1},{3,2},{4,3},{5,4},{6,5},{7,6},{8,7},{9,8},{10,9},{11,1... | collective-permute-start | bytes 393224 | tf_op jit(solution)/shard_map/while/body/eval_jaxpr/ppermute | solution.py:17
  56.4 9.8 %collective-permute-start.2 = (bf16[1024,256]{1,0:T(8,128)(2,1)S(1)}, bf16[1024,256]{1,0:T(8,128)(2,1)S(1)}, u32[]{:S(2)}, u32[]{:S(2)}) collective-permute-start(bf16[1024,256]{1,0:T(8,128)(2,1)S(1)} %bitcast.85), channel_id=1, source_target_pairs={{0,32},{32,64},{64,96},{96,128},{128,160},{160,192},{192,224},{224... | collective-permute-start | bytes 1572872 | tf_op jit(solution)/shard_map/while/body/eval_jaxpr/ppermute | solution.py:25
  66.2 7.8 %collective-permute-start = (bf16[256,256]{1,0:T(8,128)(2,1)S(1)}, bf16[256,256]{1,0:T(8,128)(2,1)S(1)}, u32[]{:S(2)}, u32[]{:S(2)}) collective-permute-start(bf16[256,256]{1,0:T(8,128)(2,1)S(1)} %get-tuple-element.117), channel_id=1, source_target_pairs={{1,0},{2,1},{3,2},{4,3},{5,4},{6,5},{7,6},{8,7},{9,8},{10,9},{11,1... | collective-permute-start | bytes 393224 | tf_op jit(solution)/shard_map/while/body/eval_jaxpr/ppermute | solution.py:17
  80.8 9.8 %collective-permute-start.2 = (bf16[1024,256]{1,0:T(8,128)(2,1)S(1)}, bf16[1024,256]{1,0:T(8,128)(2,1)S(1)}, u32[]{:S(2)}, u32[]{:S(2)}) collective-permute-start(bf16[1024,256]{1,0:T(8,128)(2,1)S(1)} %bitcast.85), channel_id=1, source_target_pairs={{0,32},{32,64},{64,96},{96,128},{128,160},{160,192},{192,224},{224... | collective-permute-start | bytes 1572872 | tf_op jit(solution)/shard_map/while/body/eval_jaxpr/ppermute | solution.py:25
  90.7 7.7 %collective-permute-start = (bf16[256,256]{1,0:T(8,128)(2,1)S(1)}, bf16[256,256]{1,0:T(8,128)(2,1)S(1)}, u32[]{:S(2)}, u32[]{:S(2)}) collective-permute-start(bf16[256,256]{1,0:T(8,128)(2,1)S(1)} %get-tuple-element.117), channel_id=1, source_target_pairs={{1,0},{2,1},{3,2},{4,3},{5,4},{6,5},{7,6},{8,7},{9,8},{10,9},{11,1... | collective-permute-start | bytes 393224 | tf_op jit(solution)/shard_map/while/body/eval_jaxpr/ppermute | solution.py:17
  105.3 9.8 %collective-permute-start.2 = (bf16[1024,256]{1,0:T(8,128)(2,1)S(1)}, bf16[1024,256]{1,0:T(8,128)(2,1)S(1)}, u32[]{:S(2)}, u32[]{:S(2)}) collective-permute-start(bf16[1024,256]{1,0:T(8,128)(2,1)S(1)} %bitcast.85), channel_id=1, source_target_pairs={{0,32},{32,64},{64,96},{96,128},{128,160},{160,192},{192,224},{224... | collective-permute-start | bytes 1572872 | tf_op jit(solution)/shard_map/while/body/eval_jaxpr/ppermute | solution.py:25
  115.1 7.8 %collective-permute-start = (bf16[256,256]{1,0:T(8,128)(2,1)S(1)}, bf16[256,256]{1,0:T(8,128)(2,1)S(1)}, u32[]{:S(2)}, u32[]{:S(2)}) collective-permute-start(bf16[256,256]{1,0:T(8,128)(2,1)S(1)} %get-tuple-element.117), channel_id=1, source_target_pairs={{1,0},{2,1},{3,2},{4,3},{5,4},{6,5},{7,6},{8,7},{9,8},{10,9},{11,1... | collective-permute-start | bytes 393224 | tf_op jit(solution)/shard_map/while/body/eval_jaxpr/ppermute | solution.py:17
  129.7 9.8 %collective-permute-start.2 = (bf16[1024,256]{1,0:T(8,128)(2,1)S(1)}, bf16[1024,256]{1,0:T(8,128)(2,1)S(1)}, u32[]{:S(2)}, u32[]{:S(2)}) collective-permute-start(bf16[1024,256]{1,0:T(8,128)(2,1)S(1)} %bitcast.85), channel_id=1, source_target_pairs={{0,32},{32,64},{64,96},{96,128},{128,160},{160,192},{192,224},{224... | collective-permute-start | bytes 1572872 | tf_op jit(solution)/shard_map/while/body/eval_jaxpr/ppermute | solution.py:25
  139.6 7.7 %collective-permute-start = (bf16[256,256]{1,0:T(8,128)(2,1)S(1)}, bf16[256,256]{1,0:T(8,128)(2,1)S(1)}, u32[]{:S(2)}, u32[]{:S(2)}) collective-permute-start(bf16[256,256]{1,0:T(8,128)(2,1)S(1)} %get-tuple-element.117), channel_id=1, source_target_pairs={{1,0},{2,1},{3,2},{4,3},{5,4},{6,5},{7,6},{8,7},{9,8},{10,9},{11,1... | collective-permute-start | bytes 393224 | tf_op jit(solution)/shard_map/while/body/eval_jaxpr/ppermute | solution.py:17
  154.2 9.8 %collective-permute-start.2 = (bf16[1024,256]{1,0:T(8,128)(2,1)S(1)}, bf16[1024,256]{1,0:T(8,128)(2,1)S(1)}, u32[]{:S(2)}, u32[]{:S(2)}) collective-permute-start(bf16[1024,256]{1,0:T(8,128)(2,1)S(1)} %bitcast.85), channel_id=1, source_target_pairs={{0,32},{32,64},{64,96},{96,128},{128,160},{160,192},{192,224},{224... | collective-permute-start | bytes 1572872 | tf_op jit(solution)/shard_map/while/body/eval_jaxpr/ppermute | solution.py:25
  164.0 7.8 %collective-permute-start = (bf16[256,256]{1,0:T(8,128)(2,1)S(1)}, bf16[256,256]{1,0:T(8,128)(2,1)S(1)}, u32[]{:S(2)}, u32[]{:S(2)}) collective-permute-start(bf16[256,256]{1,0:T(8,128)(2,1)S(1)} %get-tuple-element.117), channel_id=1, source_target_pairs={{1,0},{2,1},{3,2},{4,3},{5,4},{6,5},{7,6},{8,7},{9,8},{10,9},{11,1... | collective-permute-start | bytes 393224 | tf_op jit(solution)/shard_map/while/body/eval_jaxpr/ppermute | solution.py:17
  178.6 9.8 %collective-permute-start.2 = (bf16[1024,256]{1,0:T(8,128)(2,1)S(1)}, bf16[1024,256]{1,0:T(8,128)(2,1)S(1)}, u32[]{:S(2)}, u32[]{:S(2)}) collective-permute-start(bf16[1024,256]{1,0:T(8,128)(2,1)S(1)} %bitcast.85), channel_id=1, source_target_pairs={{0,32},{32,64},{64,96},{96,128},{128,160},{160,192},{192,224},{224... | collective-permute-start | bytes 1572872 | tf_op jit(solution)/shard_map/while/body/eval_jaxpr/ppermute | solution.py:25
  188.5 7.7 %collective-permute-start = (bf16[256,256]{1,0:T(8,128)(2,1)S(1)}, bf16[256,256]{1,0:T(8,128)(2,1)S(1)}, u32[]{:S(2)}, u32[]{:S(2)}) collective-permute-start(bf16[256,256]{1,0:T(8,128)(2,1)S(1)} %get-tuple-element.117), channel_id=1, source_target_pairs={{1,0},{2,1},{3,2},{4,3},{5,4},{6,5},{7,6},{8,7},{9,8},{10,9},{11,1... | collective-permute-start | bytes 393224 | tf_op jit(solution)/shard_map/while/body/eval_jaxpr/ppermute | solution.py:17
  203.1 9.8 %collective-permute-start.2 = (bf16[1024,256]{1,0:T(8,128)(2,1)S(1)}, bf16[1024,256]{1,0:T(8,128)(2,1)S(1)}, u32[]{:S(2)}, u32[]{:S(2)}) collective-permute-start(bf16[1024,256]{1,0:T(8,128)(2,1)S(1)} %bitcast.85), channel_id=1, source_target_pairs={{0,32},{32,64},{64,96},{96,128},{128,160},{160,192},{192,224},{224... | collective-permute-start | bytes 1572872 | tf_op jit(solution)/shard_map/while/body/eval_jaxpr/ppermute | solution.py:25
  212.9 7.8 %collective-permute-start = (bf16[256,256]{1,0:T(8,128)(2,1)S(1)}, bf16[256,256]{1,0:T(8,128)(2,1)S(1)}, u32[]{:S(2)}, u32[]{:S(2)}) collective-permute-start(bf16[256,256]{1,0:T(8,128)(2,1)S(1)} %get-tuple-element.117), channel_id=1, source_target_pairs={{1,0},{2,1},{3,2},{4,3},{5,4},{6,5},{7,6},{8,7},{9,8},{10,9},{11,1... | collective-permute-start | bytes 393224 | tf_op jit(solution)/shard_map/while/body/eval_jaxpr/ppermute | solution.py:17
  227.5 9.8 %collective-permute-start.2 = (bf16[1024,256]{1,0:T(8,128)(2,1)S(1)}, bf16[1024,256]{1,0:T(8,128)(2,1)S(1)}, u32[]{:S(2)}, u32[]{:S(2)}) collective-permute-start(bf16[1024,256]{1,0:T(8,128)(2,1)S(1)} %bitcast.85), channel_id=1, source_target_pairs={{0,32},{32,64},{64,96},{96,128},{128,160},{160,192},{192,224},{224... | collective-permute-start | bytes 1572872 | tf_op jit(solution)/shard_map/while/body/eval_jaxpr/ppermute | solution.py:25
  237.4 7.7 %collective-permute-start = (bf16[256,256]{1,0:T(8,128)(2,1)S(1)}, bf16[256,256]{1,0:T(8,128)(2,1)S(1)}, u32[]{:S(2)}, u32[]{:S(2)}) collective-permute-start(bf16[256,256]{1,0:T(8,128)(2,1)S(1)} %get-tuple-element.117), channel_id=1, source_target_pairs={{1,0},{2,1},{3,2},{4,3},{5,4},{6,5},{7,6},{8,7},{9,8},{10,9},{11,1... | collective-permute-start | bytes 393224 | tf_op jit(solution)/shard_map/while/body/eval_jaxpr/ppermute | solution.py:17
  252.0 9.8 %collective-permute-start.2 = (bf16[1024,256]{1,0:T(8,128)(2,1)S(1)}, bf16[1024,256]{1,0:T(8,128)(2,1)S(1)}, u32[]{:S(2)}, u32[]{:S(2)}) collective-permute-start(bf16[1024,256]{1,0:T(8,128)(2,1)S(1)} %bitcast.85), channel_id=1, source_target_pairs={{0,32},{32,64},{64,96},{96,128},{128,160},{160,192},{192,224},{224... | collective-permute-start | bytes 1572872 | tf_op jit(solution)/shard_map/while/body/eval_jaxpr/ppermute | solution.py:25
  261.8 7.8 %collective-permute-start = (bf16[256,256]{1,0:T(8,128)(2,1)S(1)}, bf16[256,256]{1,0:T(8,128)(2,1)S(1)}, u32[]{:S(2)}, u32[]{:S(2)}) collective-permute-start(bf16[256,256]{1,0:T(8,128)(2,1)S(1)} %get-tuple-element.117), channel_id=1, source_target_pairs={{1,0},{2,1},{3,2},{4,3},{5,4},{6,5},{7,6},{8,7},{9,8},{10,9},{11,1... | collective-permute-start | bytes 393224 | tf_op jit(solution)/shard_map/while/body/eval_jaxpr/ppermute | solution.py:17
  276.4 9.8 %collective-permute-start.2 = (bf16[1024,256]{1,0:T(8,128)(2,1)S(1)}, bf16[1024,256]{1,0:T(8,128)(2,1)S(1)}, u32[]{:S(2)}, u32[]{:S(2)}) collective-permute-start(bf16[1024,256]{1,0:T(8,128)(2,1)S(1)} %bitcast.85), channel_id=1, source_target_pairs={{0,32},{32,64},{64,96},{96,128},{128,160},{160,192},{192,224},{224... | collective-permute-start | bytes 1572872 | tf_op jit(solution)/shard_map/while/body/eval_jaxpr/ppermute | solution.py:25
  286.3 7.7 %collective-permute-start = (bf16[256,256]{1,0:T(8,128)(2,1)S(1)}, bf16[256,256]{1,0:T(8,128)(2,1)S(1)}, u32[]{:S(2)}, u32[]{:S(2)}) collective-permute-start(bf16[256,256]{1,0:T(8,128)(2,1)S(1)} %get-tuple-element.117), channel_id=1, source_target_pairs={{1,0},{2,1},{3,2},{4,3},{5,4},{6,5},{7,6},{8,7},{9,8},{10,9},{11,1... | collective-permute-start | bytes 393224 | tf_op jit(solution)/shard_map/while/body/eval_jaxpr/ppermute | solution.py:17
  300.9 9.8 %collective-permute-start.2 = (bf16[1024,256]{1,0:T(8,128)(2,1)S(1)}, bf16[1024,256]{1,0:T(8,128)(2,1)S(1)}, u32[]{:S(2)}, u32[]{:S(2)}) collective-permute-start(bf16[1024,256]{1,0:T(8,128)(2,1)S(1)} %bitcast.85), channel_id=1, source_target_pairs={{0,32},{32,64},{64,96},{96,128},{128,160},{160,192},{192,224},{224... | collective-permute-start | bytes 1572872 | tf_op jit(solution)/shard_map/while/body/eval_jaxpr/ppermute | solution.py:25
  310.7 7.8 %collective-permute-start = (bf16[256,256]{1,0:T(8,128)(2,1)S(1)}, bf16[256,256]{1,0:T(8,128)(2,1)S(1)}, u32[]{:S(2)}, u32[]{:S(2)}) collective-permute-start(bf16[256,256]{1,0:T(8,128)(2,1)S(1)} %get-tuple-element.117), channel_id=1, source_target_pairs={{1,0},{2,1},{3,2},{4,3},{5,4},{6,5},{7,6},{8,7},{9,8},{10,9},{11,1... | collective-permute-start | bytes 393224 | tf_op jit(solution)/shard_map/while/body/eval_jaxpr/ppermute | solution.py:17
  325.3 9.8 %collective-permute-start.2 = (bf16[1024,256]{1,0:T(8,128)(2,1)S(1)}, bf16[1024,256]{1,0:T(8,128)(2,1)S(1)}, u32[]{:S(2)}, u32[]{:S(2)}) collective-permute-start(bf16[1024,256]{1,0:T(8,128)(2,1)S(1)} %bitcast.85), channel_id=1, source_target_pairs={{0,32},{32,64},{64,96},{96,128},{128,160},{160,192},{192,224},{224... | collective-permute-start | bytes 1572872 | tf_op jit(solution)/shard_map/while/body/eval_jaxpr/ppermute | solution.py:25
  335.2 7.7 %collective-permute-start = (bf16[256,256]{1,0:T(8,128)(2,1)S(1)}, bf16[256,256]{1,0:T(8,128)(2,1)S(1)}, u32[]{:S(2)}, u32[]{:S(2)}) collective-permute-start(bf16[256,256]{1,0:T(8,128)(2,1)S(1)} %get-tuple-element.117), channel_id=1, source_target_pairs={{1,0},{2,1},{3,2},{4,3},{5,4},{6,5},{7,6},{8,7},{9,8},{10,9},{11,1... | collective-permute-start | bytes 393224 | tf_op jit(solution)/shard_map/while/body/eval_jaxpr/ppermute | solution.py:17
  349.7 9.8 %collective-permute-start.2 = (bf16[1024,256]{1,0:T(8,128)(2,1)S(1)}, bf16[1024,256]{1,0:T(8,128)(2,1)S(1)}, u32[]{:S(2)}, u32[]{:S(2)}) collective-permute-start(bf16[1024,256]{1,0:T(8,128)(2,1)S(1)} %bitcast.85), channel_id=1, source_target_pairs={{0,32},{32,64},{64,96},{96,128},{128,160},{160,192},{192,224},{224... | collective-permute-start | bytes 1572872 | tf_op jit(solution)/shard_map/while/body/eval_jaxpr/ppermute | solution.py:25
  359.6 7.8 %collective-permute-start = (bf16[256,256]{1,0:T(8,128)(2,1)S(1)}, bf16[256,256]{1,0:T(8,128)(2,1)S(1)}, u32[]{:S(2)}, u32[]{:S(2)}) collective-permute-start(bf16[256,256]{1,0:T(8,128)(2,1)S(1)} %get-tuple-element.117), channel_id=1, source_target_pairs={{1,0},{2,1},{3,2},{4,3},{5,4},{6,5},{7,6},{8,7},{9,8},{10,9},{11,1... | collective-permute-start | bytes 393224 | tf_op jit(solution)/shard_map/while/body/eval_jaxpr/ppermute | solution.py:17
  374.2 9.8 %collective-permute-start.2 = (bf16[1024,256]{1,0:T(8,128)(2,1)S(1)}, bf16[1024,256]{1,0:T(8,128)(2,1)S(1)}, u32[]{:S(2)}, u32[]{:S(2)}) collective-permute-start(bf16[1024,256]{1,0:T(8,128)(2,1)S(1)} %bitcast.85), channel_id=1, source_target_pairs={{0,32},{32,64},{64,96},{96,128},{128,160},{160,192},{192,224},{224... | collective-permute-start | bytes 1572872 | tf_op jit(solution)/shard_map/while/body/eval_jaxpr/ppermute | solution.py:25
  398.6 9.8 %collective-permute-start.2 = (bf16[1024,256]{1,0:T(8,128)(2,1)S(1)}, bf16[1024,256]{1,0:T(8,128)(2,1)S(1)}, u32[]{:S(2)}, u32[]{:S(2)}) collective-permute-start(bf16[1024,256]{1,0:T(8,128)(2,1)S(1)} %bitcast.85), channel_id=1, source_target_pairs={{0,32},{32,64},{64,96},{96,128},{128,160},{160,192},{192,224},{224... | collective-permute-start | bytes 1572872 | tf_op jit(solution)/shard_map/while/body/eval_jaxpr/ppermute | solution.py:25
  (19 other events, 123.9 us)
Sparse Core Ops, SparseCore 0:
  409.6 151.4 all-reduce.2
where the time goes:
time: 636 us; the launch traced here: 634 us
  waiting for transfers between devices  388 us (61%)
  starting transfers between devices  119 us (19%)
  other arithmetic  60 us (9%)
  matrix products  31.2 us (5%)
  local copies, waits for them, and re-layouts  20.1 us (3%)
  between operations  15.5 us (2%)
    ppermute x16, waiting for transfers between devices, passed_along(): return lax.ppermute(value, axis, pairs)  160 us
    psum x1, waiting for transfers between devices, body(): lax.psum(gram_term.astype(jnp.bfloat16), 'rows').astype(jnp.float32)  152 us
    ppermute x16, starting transfers between devices, with_halo(): after = lax.ppermute(leading, axis, down)  87.6 us
    ppermute x16, waiting for transfers between devices, with_halo(): before = lax.ppermute(last, axis, up)  69.8 us
    another operation x6, other arithmetic, body(): lower_factor = jnp.linalg.cholesky(gram_total)  34 us
    ppermute x16, starting transfers between devices, with_halo(): before = lax.ppermute(last, axis, up)  30.7 us
    dot_general x16, matrix products, advance(): jnp.einsum('ijab,ijbk->iak', kept_blocks, picked, preferred_element_type=...  27.7 us
    another operation x2, other arithmetic, body(): jax.scipy.linalg.solve_triangular(lower_factor, arrived.astype(jnp.float3...  19.9 us
  transfers between devices with their start and end apart: 49, of which 49 were waited for; matrix products, arithmetic and copies ran while one was open for 0% of the time, Pallas kernels for 0%

commit v1 on v0

--- a/solution.py
+++ b/solution.py
@@ -4,6 +4,7 @@
 from jax.sharding import PartitionSpec as P
 
 HB = 2
+map_leaves = lambda sheet: jnp.sum(jax.lax.all_gather(sheet, "rows"), axis=0)
 
 
 def with_halo(array, sides, width):
@@ -57,7 +58,7 @@
     gram_term = lax.dot_general(
         arrived, arrived, (((0,), (0,)), ((), ())), preferred_element_type=jnp.float32
     )
-    gram_total = lax.psum(gram_term.astype(jnp.bfloat16), "rows").astype(jnp.float32) / (
+    gram_total = map_leaves(gram_term.astype(jnp.bfloat16)).astype(jnp.float32) / (
         rows_here * owners
     )
     lower_factor = jnp.linalg.cholesky(gram_total)

time: 636 us -> 570 us (0.90)
  the two profiles are of different devices: /device:TPU:2 before, /device:TPU:8 now
where the time goes in v1:
time: 570 us; the launch traced here: 568 us
  waiting for transfers between devices  345 us (61%)
  starting transfers between devices  94.4 us (17%)
  other arithmetic  60.9 us (11%)
  matrix products  30.8 us (5%)
  local copies, waits for them, and re-layouts  20.4 us (4%)
  between operations  15.5 us (3%)
    ppermute x16, waiting for transfers between devices, passed_along(): return lax.ppermute(value, axis, pairs)  161 us
    all_gather x1, waiting for transfers between devices, jax.lax.all_gather(sheet, 'rows')  87.1 us
    ppermute x16, waiting for transfers between devices, with_halo(): before = lax.ppermute(last, axis, up)  83.8 us
    ppermute x16, starting transfers between devices, with_halo(): after = lax.ppermute(leading, axis, down)  50 us
    ppermute x16, starting transfers between devices, with_halo(): before = lax.ppermute(last, axis, up)  44.1 us
    another operation x6, other arithmetic, body(): lower_factor = jnp.linalg.cholesky(gram_total)  34 us
    dot_general x16, matrix products, advance(): jnp.einsum('ijab,ijbk->iak', kept_blocks, picked, preferred_element_type=...  27.7 us
    another operation x2, other arithmetic, body(): jax.scipy.linalg.solve_triangular(lower_factor, arrived.astype(jnp.float3...  19.9 us
  transfers between devices with their start and end apart: 49, of which 49 were waited for; matrix products, arithmetic and copies ran while one was open for 1% of the time, Pallas kernels for 0%

profile of v1, /device:TPU:8, one launch (start us, length us, event | category | flops | bytes accessed | tf_op | source)
XLA Modules:
  0.0 567.9 jit_solution(8218325077468425349)
XLA Ops:
  10.4 395.5 %while.11 = (s32[]{:T(128)}, bf16[1024,256]{1,0:T(8,128)(2,1)S(1)}, s32[8,4]{0,1:T(4,128)S(1)}, bf16[8,4,128,128]{3,2,1,0:T(8,128)(2,1)}, s32[]{:T(128)}) while((s32[]{:T(128)}, bf16[1024,256]{1,0:T(8,128)(2,1)S(1)}, s32[8,4]{0,1:T(4,128)S(1)}, bf16[8,4,128,128]{3,2,1,0:T(8,128)(2,1)}, s32[]{:T(128)}) %tuple.55), condition=%wide.region_1.2_spmd, body=%wide.region_0.1_spmd.sunk | while | flops 271058016 | bytes 13112501 | solution.py:57
  17.7 6.2 %collective-permute-done.1 = bf16[256,256]{1,0:T(8,128)(2,1)S(1)} collective-permute-done((bf16[256,256]{1,0:T(8,128)(2,1)S(1)}, bf16[256,256]{1,0:T(8,128)(2,1)S(1)}, u32[]{:S(2)}, u32[]{:S(2)}) %collective-permute-start.1) | collective-permute-done | bytes 131104 | tf_op jit(solution)/shard_map/while/body/eval_jaxpr/ppermute | solution.py:17
  26.4 13.9 %collective-permute-done.2 = bf16[1024,256]{1,0:T(8,128)(2,1)S(1)} collective-permute-done((bf16[1024,256]{1,0:T(8,128)(2,1)S(1)}, bf16[1024,256]{1,0:T(8,128)(2,1)S(1)}, u32[]{:S(2)}, u32[]{:S(2)}) %collective-permute-start.2) | collective-permute-done | bytes 524320 | tf_op jit(solution)/shard_map/while/body/eval_jaxpr/ppermute | solution.py:26
  53.8 9.8 %collective-permute-done.2 = bf16[1024,256]{1,0:T(8,128)(2,1)S(1)} collective-permute-done((bf16[1024,256]{1,0:T(8,128)(2,1)S(1)}, bf16[1024,256]{1,0:T(8,128)(2,1)S(1)}, u32[]{:S(2)}, u32[]{:S(2)}) %collective-permute-start.2) | collective-permute-done | bytes 524320 | tf_op jit(solution)/shard_map/while/body/eval_jaxpr/ppermute | solution.py:26
  77.5 9.8 %collective-permute-done.2 = bf16[1024,256]{1,0:T(8,128)(2,1)S(1)} collective-permute-done((bf16[1024,256]{1,0:T(8,128)(2,1)S(1)}, bf16[1024,256]{1,0:T(8,128)(2,1)S(1)}, u32[]{:S(2)}, u32[]{:S(2)}) %collective-permute-start.2) | collective-permute-done | bytes 524320 | tf_op jit(solution)/shard_map/while/body/eval_jaxpr/ppermute | solution.py:26
  94.2 6.0 %collective-permute-done.1 = bf16[256,256]{1,0:T(8,128)(2,1)S(1)} collective-permute-done((bf16[256,256]{1,0:T(8,128)(2,1)S(1)}, bf16[256,256]{1,0:T(8,128)(2,1)S(1)}, u32[]{:S(2)}, u32[]{:S(2)}) %collective-permute-start.1) | collective-permute-done | bytes 131104 | tf_op jit(solution)/shard_map/while/body/eval_jaxpr/ppermute | solution.py:17
  102.8 9.8 %collective-permute-done.2 = bf16[1024,256]{1,0:T(8,128)(2,1)S(1)} collective-permute-done((bf16[1024,256]{1,0:T(8,128)(2,1)S(1)}, bf16[1024,256]{1,0:T(8,128)(2,1)S(1)}, u32[]{:S(2)}, u32[]{:S(2)}) %collective-permute-start.2) | collective-permute-done | bytes 524320 | tf_op jit(solution)/shard_map/while/body/eval_jaxpr/ppermute | solution.py:26
  119.4 5.3 collective-permute-done.1
  127.2 9.8 %collective-permute-done.2 = bf16[1024,256]{1,0:T(8,128)(2,1)S(1)} collective-permute-done((bf16[1024,256]{1,0:T(8,128)(2,1)S(1)}, bf16[1024,256]{1,0:T(8,128)(2,1)S(1)}, u32[]{:S(2)}, u32[]{:S(2)}) %collective-permute-start.2) | collective-permute-done | bytes 524320 | tf_op jit(solution)/shard_map/while/body/eval_jaxpr/ppermute | solution.py:26
  143.9 5.2 collective-permute-done.1
  151.6 9.8 %collective-permute-done.2 = bf16[1024,256]{1,0:T(8,128)(2,1)S(1)} collective-permute-done((bf16[1024,256]{1,0:T(8,128)(2,1)S(1)}, bf16[1024,256]{1,0:T(8,128)(2,1)S(1)}, u32[]{:S(2)}, u32[]{:S(2)}) %collective-permute-start.2) | collective-permute-done | bytes 524320 | tf_op jit(solution)/shard_map/while/body/eval_jaxpr/ppermute | solution.py:26
  168.3 5.3 collective-permute-done.1
  176.1 9.8 %collective-permute-done.2 = bf16[1024,256]{1,0:T(8,128)(2,1)S(1)} collective-permute-done((bf16[1024,256]{1,0:T(8,128)(2,1)S(1)}, bf16[1024,256]{1,0:T(8,128)(2,1)S(1)}, u32[]{:S(2)}, u32[]{:S(2)}) %collective-permute-start.2) | collective-permute-done | bytes 524320 | tf_op jit(solution)/shard_map/while/body/eval_jaxpr/ppermute | solution.py:26
  192.8 5.2 collective-permute-done.1
  200.5 9.8 %collective-permute-done.2 = bf16[1024,256]{1,0:T(8,128)(2,1)S(1)} collective-permute-done((bf16[1024,256]{1,0:T(8,128)(2,1)S(1)}, bf16[1024,256]{1,0:T(8,128)(2,1)S(1)}, u32[]{:S(2)}, u32[]{:S(2)}) %collective-permute-start.2) | collective-permute-done | bytes 524320 | tf_op jit(solution)/shard_map/while/body/eval_jaxpr/ppermute | solution.py:26
  217.2 5.3 collective-permute-done.1
  225.0 9.8 %collective-permute-done.2 = bf16[1024,256]{1,0:T(8,128)(2,1)S(1)} collective-permute-done((bf16[1024,256]{1,0:T(8,128)(2,1)S(1)}, bf16[1024,256]{1,0:T(8,128)(2,1)S(1)}, u32[]{:S(2)}, u32[]{:S(2)}) %collective-permute-start.2) | collective-permute-done | bytes 524320 | tf_op jit(solution)/shard_map/while/body/eval_jaxpr/ppermute | solution.py:26
  249.4 9.8 %collective-permute-done.2 = bf16[1024,256]{1,0:T(8,128)(2,1)S(1)} collective-permute-done((bf16[1024,256]{1,0:T(8,128)(2,1)S(1)}, bf16[1024,256]{1,0:T(8,128)(2,1)S(1)}, u32[]{:S(2)}, u32[]{:S(2)}) %collective-permute-start.2) | collective-permute-done | bytes 524320 | tf_op jit(solution)/shard_map/while/body/eval_jaxpr/ppermute | solution.py:26
  266.1 5.3 collective-permute-done.1
  273.9 9.8 %collective-permute-done.2 = bf16[1024,256]{1,0:T(8,128)(2,1)S(1)} collective-permute-done((bf16[1024,256]{1,0:T(8,128)(2,1)S(1)}, bf16[1024,256]{1,0:T(8,128)(2,1)S(1)}, u32[]{:S(2)}, u32[]{:S(2)}) %collective-permute-start.2) | collective-permute-done | bytes 524320 | tf_op jit(solution)/shard_map/while/body/eval_jaxpr/ppermute | solution.py:26
  298.3 9.8 %collective-permute-done.2 = bf16[1024,256]{1,0:T(8,128)(2,1)S(1)} collective-permute-done((bf16[1024,256]{1,0:T(8,128)(2,1)S(1)}, bf16[1024,256]{1,0:T(8,128)(2,1)S(1)}, u32[]{:S(2)}, u32[]{:S(2)}) %collective-permute-start.2) | collective-permute-done | bytes 524320 | tf_op jit(solution)/shard_map/while/body/eval_jaxpr/ppermute | solution.py:26
  315.0 5.3 collective-permute-done.1
  322.8 9.8 %collective-permute-done.2 = bf16[1024,256]{1,0:T(8,128)(2,1)S(1)} collective-permute-done((bf16[1024,256]{1,0:T(8,128)(2,1)S(1)}, bf16[1024,256]{1,0:T(8,128)(2,1)S(1)}, u32[]{:S(2)}, u32[]{:S(2)}) %collective-permute-start.2) | collective-permute-done | bytes 524320 | tf_op jit(solution)/shard_map/while/body/eval_jaxpr/ppermute | solution.py:26
  347.2 9.8 %collective-permute-done.2 = bf16[1024,256]{1,0:T(8,128)(2,1)S(1)} collective-permute-done((bf16[1024,256]{1,0:T(8,128)(2,1)S(1)}, bf16[1024,256]{1,0:T(8,128)(2,1)S(1)}, u32[]{:S(2)}, u32[]{:S(2)}) %collective-permute-start.2) | collective-permute-done | bytes 524320 | tf_op jit(solution)/shard_map/while/body/eval_jaxpr/ppermute | solution.py:26
  363.9 5.3 collective-permute-done.1
  371.7 9.8 %collective-permute-done.2 = bf16[1024,256]{1,0:T(8,128)(2,1)S(1)} collective-permute-done((bf16[1024,256]{1,0:T(8,128)(2,1)S(1)}, bf16[1024,256]{1,0:T(8,128)(2,1)S(1)}, u32[]{:S(2)}, u32[]{:S(2)}) %collective-permute-start.2) | collective-permute-done | bytes 524320 | tf_op jit(solution)/shard_map/while/body/eval_jaxpr/ppermute | solution.py:26
  396.1 9.8 %collective-permute-done.2 = bf16[1024,256]{1,0:T(8,128)(2,1)S(1)} collective-permute-done((bf16[1024,256]{1,0:T(8,128)(2,1)S(1)}, bf16[1024,256]{1,0:T(8,128)(2,1)S(1)}, u32[]{:S(2)}, u32[]{:S(2)}) %collective-permute-start.2) | collective-permute-done | bytes 524320 | tf_op jit(solution)/shard_map/while/body/eval_jaxpr/ppermute | solution.py:26
  407.2 87.1 %all-gather.3.cloned.1.call-done = bf16[8192,256]{1,0:T(8,128)(2,1)} async-done(((bf16[256,256]{1,0:T(8,128)(2,1)}), bf16[8192,256]{1,0:T(8,128)(2,1)}) %all-gather.3.cloned.1.call-update) | async-done | bytes 4194320 | tf_op jit(solution)/shard_map/all_gather | solution.py:7
  497.4 11.7 %cholesky.50 = f32[128,128]{1,0:T(8,128)S(1)} custom-call(f32[128,128]{1,0:T(8,128)S(1)} %cholesky.118), custom_call_target="Cholesky" | custom-call | tf_op jit(solution)/shard_map/jit(cholesky)/cholesky | solution.py:64
  509.1 9.8 %custom-call.15 = f32[1,128,128]{1,2,0:T(8,128)S(1)} custom-call(f32[1,128,128]{2,1,0:T(8,128)S(1)} %get-tuple-element.64), custom_call_target="InvertDiagBlocksLowerTriangular" | custom-call | tf_op jit(solution)/shard_map/jit(cholesky)/cholesky | solution.py:64
  519.4 11.7 %cholesky.105 = f32[128,128]{1,0:T(8,128)S(1)} custom-call(f32[128,128]{1,0:T(8,128)S(1)} %convolution_subtract_fusion.1), custom_call_target="Cholesky" | custom-call | tf_op jit(solution)/shard_map/jit(cholesky)/cholesky | solution.py:64
  537.2 19.9 %custom-call.16 = f32[2,128,128]{1,2,0:T(8,128)S(1)} custom-call(f32[2,128,128]{2,1,0:T(8,128)S(1)} %get-tuple-element.32), custom_call_target="InvertDiagBlocksLowerTriangular" | custom-call | tf_op jit(solution)/shard_map/jit(_solve_triangular)/triangular_solve | solution.py:65
  (237 shorter events, 199.9 us)
Async XLA Ops:
  7.2 487.1 %all-gather.3.cloned.1.call-start = ((), (), s32[]{:S(2)}) async-start(), calls=%async_computation | async-start | bytes 4325376 | tf_op jit(solution)/shard_map/all_gather | solution.py:7
  15.0 9.0 %collective-permute-start.1 = (bf16[256,256]{1,0:T(8,128)(2,1)S(1)}, bf16[256,256]{1,0:T(8,128)(2,1)S(1)}, u32[]{:S(2)}, u32[]{:S(2)}) collective-permute-start(bf16[256,256]{1,0:T(8,128)(2,1)S(1)} %get-tuple-element.120), channel_id=1, source_target_pairs={{0,1},{1,2},{2,3},{3,4},{4,5},{5,6},{6,7},{7,8},{8,9},{9,10},{10,1... | collective-permute-start | bytes 393224 | tf_op jit(solution)/shard_map/while/body/eval_jaxpr/ppermute | solution.py:17
  26.4 13.9 %collective-permute-start.2 = (bf16[1024,256]{1,0:T(8,128)(2,1)S(1)}, bf16[1024,256]{1,0:T(8,128)(2,1)S(1)}, u32[]{:S(2)}, u32[]{:S(2)}) collective-permute-start(bf16[1024,256]{1,0:T(8,128)(2,1)S(1)} %bitcast.84), channel_id=1, source_target_pairs={{0,32},{32,64},{64,96},{96,128},{128,160},{160,192},{192,224},{224... | collective-permute-start | bytes 1572872 | tf_op jit(solution)/shard_map/while/body/eval_jaxpr/ppermute | solution.py:26
  42.3 9.0 %collective-permute-start.1 = (bf16[256,256]{1,0:T(8,128)(2,1)S(1)}, bf16[256,256]{1,0:T(8,128)(2,1)S(1)}, u32[]{:S(2)}, u32[]{:S(2)}) collective-permute-start(bf16[256,256]{1,0:T(8,128)(2,1)S(1)} %get-tuple-element.120), channel_id=1, source_target_pairs={{0,1},{1,2},{2,3},{3,4},{4,5},{5,6},{6,7},{7,8},{8,9},{9,10},{10,1... | collective-permute-start | bytes 393224 | tf_op jit(solution)/shard_map/while/body/eval_jaxpr/ppermute | solution.py:17
  53.8 9.8 %collective-permute-start.2 = (bf16[1024,256]{1,0:T(8,128)(2,1)S(1)}, bf16[1024,256]{1,0:T(8,128)(2,1)S(1)}, u32[]{:S(2)}, u32[]{:S(2)}) collective-permute-start(bf16[1024,256]{1,0:T(8,128)(2,1)S(1)} %bitcast.84), channel_id=1, source_target_pairs={{0,32},{32,64},{64,96},{96,128},{128,160},{160,192},{192,224},{224... | collective-permute-start | bytes 1572872 | tf_op jit(solution)/shard_map/while/body/eval_jaxpr/ppermute | solution.py:26
  65.7 9.3 %collective-permute-start.1 = (bf16[256,256]{1,0:T(8,128)(2,1)S(1)}, bf16[256,256]{1,0:T(8,128)(2,1)S(1)}, u32[]{:S(2)}, u32[]{:S(2)}) collective-permute-start(bf16[256,256]{1,0:T(8,128)(2,1)S(1)} %get-tuple-element.120), channel_id=1, source_target_pairs={{0,1},{1,2},{2,3},{3,4},{4,5},{5,6},{6,7},{7,8},{8,9},{9,10},{10,1... | collective-permute-start | bytes 393224 | tf_op jit(solution)/shard_map/while/body/eval_jaxpr/ppermute | solution.py:17
  77.5 9.8 %collective-permute-start.2 = (bf16[1024,256]{1,0:T(8,128)(2,1)S(1)}, bf16[1024,256]{1,0:T(8,128)(2,1)S(1)}, u32[]{:S(2)}, u32[]{:S(2)}) collective-permute-start(bf16[1024,256]{1,0:T(8,128)(2,1)S(1)} %bitcast.84), channel_id=1, source_target_pairs={{0,32},{32,64},{64,96},{96,128},{128,160},{160,192},{192,224},{224... | collective-permute-start | bytes 1572872 | tf_op jit(solution)/shard_map/while/body/eval_jaxpr/ppermute | solution.py:26
  91.3 9.0 %collective-permute-start.1 = (bf16[256,256]{1,0:T(8,128)(2,1)S(1)}, bf16[256,256]{1,0:T(8,128)(2,1)S(1)}, u32[]{:S(2)}, u32[]{:S(2)}) collective-permute-start(bf16[256,256]{1,0:T(8,128)(2,1)S(1)} %get-tuple-element.120), channel_id=1, source_target_pairs={{0,1},{1,2},{2,3},{3,4},{4,5},{5,6},{6,7},{7,8},{8,9},{9,10},{10,1... | collective-permute-start | bytes 393224 | tf_op jit(solution)/shard_map/while/body/eval_jaxpr/ppermute | solution.py:17
  102.7 9.8 %collective-permute-start.2 = (bf16[1024,256]{1,0:T(8,128)(2,1)S(1)}, bf16[1024,256]{1,0:T(8,128)(2,1)S(1)}, u32[]{:S(2)}, u32[]{:S(2)}) collective-permute-start(bf16[1024,256]{1,0:T(8,128)(2,1)S(1)} %bitcast.84), channel_id=1, source_target_pairs={{0,32},{32,64},{64,96},{96,128},{128,160},{160,192},{192,224},{224... | collective-permute-start | bytes 1572872 | tf_op jit(solution)/shard_map/while/body/eval_jaxpr/ppermute | solution.py:26
  115.7 9.0 %collective-permute-start.1 = (bf16[256,256]{1,0:T(8,128)(2,1)S(1)}, bf16[256,256]{1,0:T(8,128)(2,1)S(1)}, u32[]{:S(2)}, u32[]{:S(2)}) collective-permute-start(bf16[256,256]{1,0:T(8,128)(2,1)S(1)} %get-tuple-element.120), channel_id=1, source_target_pairs={{0,1},{1,2},{2,3},{3,4},{4,5},{5,6},{6,7},{7,8},{8,9},{9,10},{10,1... | collective-permute-start | bytes 393224 | tf_op jit(solution)/shard_map/while/body/eval_jaxpr/ppermute | solution.py:17
  127.2 9.8 %collective-permute-start.2 = (bf16[1024,256]{1,0:T(8,128)(2,1)S(1)}, bf16[1024,256]{1,0:T(8,128)(2,1)S(1)}, u32[]{:S(2)}, u32[]{:S(2)}) collective-permute-start(bf16[1024,256]{1,0:T(8,128)(2,1)S(1)} %bitcast.84), channel_id=1, source_target_pairs={{0,32},{32,64},{64,96},{96,128},{128,160},{160,192},{192,224},{224... | collective-permute-start | bytes 1572872 | tf_op jit(solution)/shard_map/while/body/eval_jaxpr/ppermute | solution.py:26
  140.2 9.0 %collective-permute-start.1 = (bf16[256,256]{1,0:T(8,128)(2,1)S(1)}, bf16[256,256]{1,0:T(8,128)(2,1)S(1)}, u32[]{:S(2)}, u32[]{:S(2)}) collective-permute-start(bf16[256,256]{1,0:T(8,128)(2,1)S(1)} %get-tuple-element.120), channel_id=1, source_target_pairs={{0,1},{1,2},{2,3},{3,4},{4,5},{5,6},{6,7},{7,8},{8,9},{9,10},{10,1... | collective-permute-start | bytes 393224 | tf_op jit(solution)/shard_map/while/body/eval_jaxpr/ppermute | solution.py:17
  151.6 9.8 %collective-permute-start.2 = (bf16[1024,256]{1,0:T(8,128)(2,1)S(1)}, bf16[1024,256]{1,0:T(8,128)(2,1)S(1)}, u32[]{:S(2)}, u32[]{:S(2)}) collective-permute-start(bf16[1024,256]{1,0:T(8,128)(2,1)S(1)} %bitcast.84), channel_id=1, source_target_pairs={{0,32},{32,64},{64,96},{96,128},{128,160},{160,192},{192,224},{224... | collective-permute-start | bytes 1572872 | tf_op jit(solution)/shard_map/while/body/eval_jaxpr/ppermute | solution.py:26
  164.6 9.0 %collective-permute-start.1 = (bf16[256,256]{1,0:T(8,128)(2,1)S(1)}, bf16[256,256]{1,0:T(8,128)(2,1)S(1)}, u32[]{:S(2)}, u32[]{:S(2)}) collective-permute-start(bf16[256,256]{1,0:T(8,128)(2,1)S(1)} %get-tuple-element.120), channel_id=1, source_target_pairs={{0,1},{1,2},{2,3},{3,4},{4,5},{5,6},{6,7},{7,8},{8,9},{9,10},{10,1... | collective-permute-start | bytes 393224 | tf_op jit(solution)/shard_map/while/body/eval_jaxpr/ppermute | solution.py:17
  176.1 9.8 %collective-permute-start.2 = (bf16[1024,256]{1,0:T(8,128)(2,1)S(1)}, bf16[1024,256]{1,0:T(8,128)(2,1)S(1)}, u32[]{:S(2)}, u32[]{:S(2)}) collective-permute-start(bf16[1024,256]{1,0:T(8,128)(2,1)S(1)} %bitcast.84), channel_id=1, source_target_pairs={{0,32},{32,64},{64,96},{96,128},{128,160},{160,192},{192,224},{224... | collective-permute-start | bytes 1572872 | tf_op jit(solution)/shard_map/while/body/eval_jaxpr/ppermute | solution.py:26
  189.0 9.0 %collective-permute-start.1 = (bf16[256,256]{1,0:T(8,128)(2,1)S(1)}, bf16[256,256]{1,0:T(8,128)(2,1)S(1)}, u32[]{:S(2)}, u32[]{:S(2)}) collective-permute-start(bf16[256,256]{1,0:T(8,128)(2,1)S(1)} %get-tuple-element.120), channel_id=1, source_target_pairs={{0,1},{1,2},{2,3},{3,4},{4,5},{5,6},{6,7},{7,8},{8,9},{9,10},{10,1... | collective-permute-start | bytes 393224 | tf_op jit(solution)/shard_map/while/body/eval_jaxpr/ppermute | solution.py:17
  200.5 9.8 %collective-permute-start.2 = (bf16[1024,256]{1,0:T(8,128)(2,1)S(1)}, bf16[1024,256]{1,0:T(8,128)(2,1)S(1)}, u32[]{:S(2)}, u32[]{:S(2)}) collective-permute-start(bf16[1024,256]{1,0:T(8,128)(2,1)S(1)} %bitcast.84), channel_id=1, source_target_pairs={{0,32},{32,64},{64,96},{96,128},{128,160},{160,192},{192,224},{224... | collective-permute-start | bytes 1572872 | tf_op jit(solution)/shard_map/while/body/eval_jaxpr/ppermute | solution.py:26
  213.5 9.0 %collective-permute-start.1 = (bf16[256,256]{1,0:T(8,128)(2,1)S(1)}, bf16[256,256]{1,0:T(8,128)(2,1)S(1)}, u32[]{:S(2)}, u32[]{:S(2)}) collective-permute-start(bf16[256,256]{1,0:T(8,128)(2,1)S(1)} %get-tuple-element.120), channel_id=1, source_target_pairs={{0,1},{1,2},{2,3},{3,4},{4,5},{5,6},{6,7},{7,8},{8,9},{9,10},{10,1... | collective-permute-start | bytes 393224 | tf_op jit(solution)/shard_map/while/body/eval_jaxpr/ppermute | solution.py:17
  225.0 9.8 %collective-permute-start.2 = (bf16[1024,256]{1,0:T(8,128)(2,1)S(1)}, bf16[1024,256]{1,0:T(8,128)(2,1)S(1)}, u32[]{:S(2)}, u32[]{:S(2)}) collective-permute-start(bf16[1024,256]{1,0:T(8,128)(2,1)S(1)} %bitcast.84), channel_id=1, source_target_pairs={{0,32},{32,64},{64,96},{96,128},{128,160},{160,192},{192,224},{224... | collective-permute-start | bytes 1572872 | tf_op jit(solution)/shard_map/while/body/eval_jaxpr/ppermute | solution.py:26
  237.9 9.0 %collective-permute-start.1 = (bf16[256,256]{1,0:T(8,128)(2,1)S(1)}, bf16[256,256]{1,0:T(8,128)(2,1)S(1)}, u32[]{:S(2)}, u32[]{:S(2)}) collective-permute-start(bf16[256,256]{1,0:T(8,128)(2,1)S(1)} %get-tuple-element.120), channel_id=1, source_target_pairs={{0,1},{1,2},{2,3},{3,4},{4,5},{5,6},{6,7},{7,8},{8,9},{9,10},{10,1... | collective-permute-start | bytes 393224 | tf_op jit(solution)/shard_map/while/body/eval_jaxpr/ppermute | solution.py:17
  249.4 9.8 %collective-permute-start.2 = (bf16[1024,256]{1,0:T(8,128)(2,1)S(1)}, bf16[1024,256]{1,0:T(8,128)(2,1)S(1)}, u32[]{:S(2)}, u32[]{:S(2)}) collective-permute-start(bf16[1024,256]{1,0:T(8,128)(2,1)S(1)} %bitcast.84), channel_id=1, source_target_pairs={{0,32},{32,64},{64,96},{96,128},{128,160},{160,192},{192,224},{224... | collective-permute-start | bytes 1572872 | tf_op jit(solution)/shard_map/while/body/eval_jaxpr/ppermute | solution.py:26
  262.4 9.0 %collective-permute-start.1 = (bf16[256,256]{1,0:T(8,128)(2,1)S(1)}, bf16[256,256]{1,0:T(8,128)(2,1)S(1)}, u32[]{:S(2)}, u32[]{:S(2)}) collective-permute-start(bf16[256,256]{1,0:T(8,128)(2,1)S(1)} %get-tuple-element.120), channel_id=1, source_target_pairs={{0,1},{1,2},{2,3},{3,4},{4,5},{5,6},{6,7},{7,8},{8,9},{9,10},{10,1... | collective-permute-start | bytes 393224 | tf_op jit(solution)/shard_map/while/body/eval_jaxpr/ppermute | solution.py:17
  273.8 9.8 %collective-permute-start.2 = (bf16[1024,256]{1,0:T(8,128)(2,1)S(1)}, bf16[1024,256]{1,0:T(8,128)(2,1)S(1)}, u32[]{:S(2)}, u32[]{:S(2)}) collective-permute-start(bf16[1024,256]{1,0:T(8,128)(2,1)S(1)} %bitcast.84), channel_id=1, source_target_pairs={{0,32},{32,64},{64,96},{96,128},{128,160},{160,192},{192,224},{224... | collective-permute-start | bytes 1572872 | tf_op jit(solution)/shard_map/while/body/eval_jaxpr/ppermute | solution.py:26
  286.8 9.0 %collective-permute-start.1 = (bf16[256,256]{1,0:T(8,128)(2,1)S(1)}, bf16[256,256]{1,0:T(8,128)(2,1)S(1)}, u32[]{:S(2)}, u32[]{:S(2)}) collective-permute-start(bf16[256,256]{1,0:T(8,128)(2,1)S(1)} %get-tuple-element.120), channel_id=1, source_target_pairs={{0,1},{1,2},{2,3},{3,4},{4,5},{5,6},{6,7},{7,8},{8,9},{9,10},{10,1... | collective-permute-start | bytes 393224 | tf_op jit(solution)/shard_map/while/body/eval_jaxpr/ppermute | solution.py:17
  298.3 9.8 %collective-permute-start.2 = (bf16[1024,256]{1,0:T(8,128)(2,1)S(1)}, bf16[1024,256]{1,0:T(8,128)(2,1)S(1)}, u32[]{:S(2)}, u32[]{:S(2)}) collective-permute-start(bf16[1024,256]{1,0:T(8,128)(2,1)S(1)} %bitcast.84), channel_id=1, source_target_pairs={{0,32},{32,64},{64,96},{96,128},{128,160},{160,192},{192,224},{224... | collective-permute-start | bytes 1572872 | tf_op jit(solution)/shard_map/while/body/eval_jaxpr/ppermute | solution.py:26
  311.3 9.0 %collective-permute-start.1 = (bf16[256,256]{1,0:T(8,128)(2,1)S(1)}, bf16[256,256]{1,0:T(8,128)(2,1)S(1)}, u32[]{:S(2)}, u32[]{:S(2)}) collective-permute-start(bf16[256,256]{1,0:T(8,128)(2,1)S(1)} %get-tuple-element.120), channel_id=1, source_target_pairs={{0,1},{1,2},{2,3},{3,4},{4,5},{5,6},{6,7},{7,8},{8,9},{9,10},{10,1... | collective-permute-start | bytes 393224 | tf_op jit(solution)/shard_map/while/body/eval_jaxpr/ppermute | solution.py:17
  322.7 9.8 %collective-permute-start.2 = (bf16[1024,256]{1,0:T(8,128)(2,1)S(1)}, bf16[1024,256]{1,0:T(8,128)(2,1)S(1)}, u32[]{:S(2)}, u32[]{:S(2)}) collective-permute-start(bf16[1024,256]{1,0:T(8,128)(2,1)S(1)} %bitcast.84), channel_id=1, source_target_pairs={{0,32},{32,64},{64,96},{96,128},{128,160},{160,192},{192,224},{224... | collective-permute-start | bytes 1572872 | tf_op jit(solution)/shard_map/while/body/eval_jaxpr/ppermute | solution.py:26
  335.7 9.0 %collective-permute-start.1 = (bf16[256,256]{1,0:T(8,128)(2,1)S(1)}, bf16[256,256]{1,0:T(8,128)(2,1)S(1)}, u32[]{:S(2)}, u32[]{:S(2)}) collective-permute-start(bf16[256,256]{1,0:T(8,128)(2,1)S(1)} %get-tuple-element.120), channel_id=1, source_target_pairs={{0,1},{1,2},{2,3},{3,4},{4,5},{5,6},{6,7},{7,8},{8,9},{9,10},{10,1... | collective-permute-start | bytes 393224 | tf_op jit(solution)/shard_map/while/body/eval_jaxpr/ppermute | solution.py:17
  347.2 9.8 %collective-permute-start.2 = (bf16[1024,256]{1,0:T(8,128)(2,1)S(1)}, bf16[1024,256]{1,0:T(8,128)(2,1)S(1)}, u32[]{:S(2)}, u32[]{:S(2)}) collective-permute-start(bf16[1024,256]{1,0:T(8,128)(2,1)S(1)} %bitcast.84), channel_id=1, source_target_pairs={{0,32},{32,64},{64,96},{96,128},{128,160},{160,192},{192,224},{224... | collective-permute-start | bytes 1572872 | tf_op jit(solution)/shard_map/while/body/eval_jaxpr/ppermute | solution.py:26
  360.2 9.0 %collective-permute-start.1 = (bf16[256,256]{1,0:T(8,128)(2,1)S(1)}, bf16[256,256]{1,0:T(8,128)(2,1)S(1)}, u32[]{:S(2)}, u32[]{:S(2)}) collective-permute-start(bf16[256,256]{1,0:T(8,128)(2,1)S(1)} %get-tuple-element.120), channel_id=1, source_target_pairs={{0,1},{1,2},{2,3},{3,4},{4,5},{5,6},{6,7},{7,8},{8,9},{9,10},{10,1... | collective-permute-start | bytes 393224 | tf_op jit(solution)/shard_map/while/body/eval_jaxpr/ppermute | solution.py:17
  371.6 9.8 %collective-permute-start.2 = (bf16[1024,256]{1,0:T(8,128)(2,1)S(1)}, bf16[1024,256]{1,0:T(8,128)(2,1)S(1)}, u32[]{:S(2)}, u32[]{:S(2)}) collective-permute-start(bf16[1024,256]{1,0:T(8,128)(2,1)S(1)} %bitcast.84), channel_id=1, source_target_pairs={{0,32},{32,64},{64,96},{96,128},{128,160},{160,192},{192,224},{224... | collective-permute-start | bytes 1572872 | tf_op jit(solution)/shard_map/while/body/eval_jaxpr/ppermute | solution.py:26
  396.1 9.8 %collective-permute-start.2 = (bf16[1024,256]{1,0:T(8,128)(2,1)S(1)}, bf16[1024,256]{1,0:T(8,128)(2,1)S(1)}, u32[]{:S(2)}, u32[]{:S(2)}) collective-permute-start(bf16[1024,256]{1,0:T(8,128)(2,1)S(1)} %bitcast.84), channel_id=1, source_target_pairs={{0,32},{32,64},{64,96},{96,128},{128,160},{160,192},{192,224},{224... | collective-permute-start | bytes 1572872 | tf_op jit(solution)/shard_map/while/body/eval_jaxpr/ppermute | solution.py:26
  (19 other events, 125.6 us)
Sparse Core Ops, SparseCore 0:
  407.1 87.1 all-gather.2
